TPU v7x, 32 devices: a whole 2x2x4 slice. The times are simulated.
32 devices in a mesh: gx: 16 (over z, y, x), gy: 2 (over core).
Axes of the slice: x: 2, y: 2, z: 4, core: 2. Of those that a mesh axis runs over, the one named last changes fastest.
Arguments:
- density: float32 [128, 32, 64], P('gx', None, 'gy'), may hold values from 0.5 to 1.5
- momentum: float32 [3, 128, 32, 64], P(None, 'gx', None, 'gy'), may hold values from -3 to 3
- energy: float32 [128, 32, 64], P('gx', None, 'gy'), may hold values from 2.5 to 4
- eddy_normal_cell: int32 [1024], P('gx'), may hold values from 0 to 63
- eddy_spanwise_cell: int32 [1024], P('gx'), may hold values from 0 to 31
- eddy_signs: int32 [1024, 3], P('gx'), may hold values from 0 to 1
- eddy_strengths: float32 [1024], P('gx'), may hold values from 0.3 to 3
- filter_matrices: float32 [1, 128, 128], replicated, may hold values from -1.25 to 1.25
- shock_switch: int32 [1, 64], P(None, 'gy'), may hold values 0 or 1
- dilatation_bin: int32 [128, 32, 64], P('gx', None, 'gy'), may hold values from 0 to 63
- vorticity_bin: int32 [128, 32, 64], P('gx', None, 'gy'), may hold values from 0 to 63, as said below
Outputs:
- conserved_next: float32 [5, 128, 32, 64], P(None, 'gx', None, 'gy')
- histogram: float32 [64, 64], replicated
Inputs may be any that keep to these rules, and one draw needn't show every extreme that they name: vorticity_bin at streamwise cell x is x * 64 // 128 or one more, modulo 64.
All inputs are finite; a program needn't handle non-finite values. No bound on the sum of `shock_switch` on one device may be relied on, other than what follows from the above.
Results may differ from a plain program's by a relative error of at most 0.0003.
Values sent between devices are 32-bit elements; how exact they have to be, the bound alone decides.
No kernel may reach another device: no remote copies, remote signals or barrier semaphores. Data moves between devices by JAX's collectives and lax.ppermute only.
A program may use at most 64 MiB of HBM per device.

v0:
```python
import math
import jax
import jax.numpy as jnp
from jax import lax
from jax.sharding import PartitionSpec as P

HISTOGRAM_BINS = 64
SIGMA_Y = 32
SIGMA_Z = 8
TIME_STEP = 0.1
GAMMA_GAS = 1.4
SENSOR_EPS = 0.1
HAT_PEAK = math.sqrt(1.5)


def extended(x, sides, width):
    for axis, dim in sides:
        size, length = (lax.axis_size(axis), x.shape[dim])
        up = [(i, (i + 1) % size) for i in range(size - 1)]
        down = [(j, i) for i, j in up]
        last = lax.slice_in_dim(x, length - width, length, axis=dim)
        first = lax.slice_in_dim(x, 0, width, axis=dim)
        before = lax.ppermute(last, axis, up)
        after = lax.ppermute(first, axis, down)
        x = jnp.concatenate([before, x, after], axis=dim)
    return x


def hat_shape(centres, coords, spread, period):
    offset = coords[None, :] - centres[:, None]
    if period > 0:
        offset = jnp.mod(offset + period / 2, period) - period / 2
    return HAT_PEAK * jnp.maximum(0.0, 1.0 - jnp.abs(offset) / spread)


def inflow_from(centre_y, centre_z, eddy_weight, coords_y, coords_z, span):
    shape_y = hat_shape(centre_y, coords_y, float(SIGMA_Y), 0)
    shape_z = hat_shape(centre_z, coords_z, float(SIGMA_Z), span)
    weighted = (eddy_weight[:, :, None] * shape_z[:, None, :]).reshape(eddy_weight.shape[0], -1)
    inflow = jnp.dot(weighted.T, shape_y, precision=lax.Precision.HIGHEST)
    return inflow.reshape(3, coords_z.shape[0], coords_y.shape[0])


def ghost_state(inflow):
    mom_x = 1.0 + inflow[0]
    kinetic = mom_x * mom_x + inflow[1] * inflow[1] + inflow[2] * inflow[2]
    return jnp.stack([jnp.ones_like(mom_x), mom_x, inflow[1], inflow[2], 3.0 + 0.5 * kinetic])


def flux_of(fields, velocity, pressure, direction):
    result = fields * velocity[direction][None]
    result = result.at[1 + direction].add(pressure)
    return result.at[4].add(pressure * velocity[direction])


def central_x(values):
    return (values[..., 2:, :, 1:-1] - values[..., :-2, :, 1:-1]) * 0.5


def central_y(values):
    return (values[..., 1:-1, :, 2:] - values[..., 1:-1, :, :-2]) * 0.5


def central_z(values):
    centre = values[..., 1:-1, :, 1:-1]
    return (jnp.roll(centre, -1, axis=-2) - jnp.roll(centre, 1, axis=-2)) * 0.5


def section_rhs(padded):
    velocity = padded[1:4] / padded[0][None]
    pressure = (GAMMA_GAS - 1.0) * (padded[4] - 0.5 * jnp.sum(padded[1:4] * velocity, axis=0))
    change = central_x(flux_of(padded, velocity, pressure, 0))
    change = change + central_y(flux_of(padded, velocity, pressure, 1))
    change = change + central_z(flux_of(padded, velocity, pressure, 2))
    updated = padded[:, 1:-1, :, 1:-1] - TIME_STEP * change
    dilatation = central_x(velocity[0]) + central_y(velocity[1]) + central_z(velocity[2])
    vort_x = central_y(velocity[2]) - central_z(velocity[1])
    vort_y = central_z(velocity[0]) - central_x(velocity[2])
    vort_z = central_x(velocity[1]) - central_y(velocity[0])
    squared = dilatation * dilatation
    shock_sensor = squared / (
        squared + vort_x * vort_x + vort_y * vort_y + vort_z * vort_z + SENSOR_EPS
    )
    return (updated, shock_sensor)


def filter_lines(pencil, filter_matrices):
    block_count, block_len = (filter_matrices.shape[0], filter_matrices.shape[1])
    lanes = pencil.shape[2]
    blocks = pencil.reshape(5, block_count, block_len, lanes)
    smooth = jnp.einsum("bij,fbjp->fbip", filter_matrices, blocks, precision=lax.Precision.HIGHEST)
    return smooth.reshape(5, block_count * block_len, lanes)


def plane_histogram(shock_sensor, dilatation_bin, vorticity_bin):
    bin_levels = jnp.arange(HISTOGRAM_BINS, dtype=jnp.int32)

    def accumulate_plane(histogram_totals, histogram_parts):
        sensor_plane, plane_dilatation, plane_vorticity = histogram_parts
        flat_sensor = sensor_plane.reshape(-1)
        dilatation_table = (plane_dilatation.reshape(-1)[None, :] == bin_levels[:, None]).astype(
            jnp.float32
        )
        vorticity_table = jnp.where(
            plane_vorticity.reshape(-1)[:, None] == bin_levels[None, :], flat_sensor[:, None], 0.0
        )
        return (
            histogram_totals
            + jnp.dot(dilatation_table, vorticity_table, precision=lax.Precision.HIGHEST),
            None,
        )

    histogram_totals, _ = lax.scan(
        accumulate_plane,
        jnp.zeros((HISTOGRAM_BINS, HISTOGRAM_BINS), jnp.float32),
        (shock_sensor, dilatation_bin, vorticity_bin),
    )
    return histogram_totals


def shards(
    density,
    momentum,
    energy,
    eddy_normal_cell,
    eddy_spanwise_cell,
    eddy_signs,
    eddy_strengths,
    filter_matrices,
    shock_switch,
    dilatation_bin,
    vorticity_bin,
):
    cells_x, span, cells_y = density.shape
    slab_index = lax.axis_index("gx")
    block_index = lax.axis_index("gy")
    slab_count = lax.axis_size("gx")
    fields = jnp.concatenate([density[None], momentum, energy[None]], axis=0)
    total_y = cells_y * lax.axis_size("gy")
    total_eddies = eddy_normal_cell.shape[0] * slab_count
    amplitude = math.sqrt(total_y * span / (total_eddies * SIGMA_Y * SIGMA_Z))
    eddy_weight = (2 * eddy_signs - 1).astype(jnp.float32) * eddy_strengths[:, None] * amplitude
    coords_y = (block_index * cells_y + jnp.arange(cells_y, dtype=jnp.int32)).astype(jnp.float32)
    coords_z = jnp.arange(span, dtype=jnp.int32).astype(jnp.float32)
    partial_sum = inflow_from(
        eddy_normal_cell.astype(jnp.float32),
        eddy_spanwise_cell.astype(jnp.float32),
        eddy_weight,
        coords_y,
        coords_z,
        span,
    )
    inflow = lax.psum(partial_sum, "gx")
    ghost_cells = ghost_state(inflow)
    padded = extended(fields, (("gx", 1), ("gy", 3)), 1)
    padded = padded.at[:, 0, :, 1:-1].set(
        jnp.where(slab_index == 0, ghost_cells, padded[:, 0, :, 1:-1])
    )
    padded = padded.at[:, -1, :, 1:-1].set(
        jnp.where(slab_index == slab_count - 1, fields[:, -1], padded[:, -1, :, 1:-1])
    )
    padded = padded.at[:, 1:-1, :, 0].set(
        jnp.where(block_index == 0, fields[:, :, :, 0], padded[:, 1:-1, :, 0])
    )
    padded = padded.at[:, 1:-1, :, -1].set(
        jnp.where(
            block_index == lax.axis_size("gy") - 1, fields[:, :, :, -1], padded[:, 1:-1, :, -1]
        )
    )
    updated, shock_sensor = section_rhs(padded)
    block_len = filter_matrices.shape[1]
    filter_row = slab_index * cells_x // block_len
    mask_row = lax.dynamic_slice_in_dim(shock_switch, filter_row, 1, 0).astype(jnp.float32)
    weight = mask_row[None] * shock_sensor
    columns = span * cells_y
    stacked = updated.reshape(5, cells_x, columns)
    weight_flat = weight.reshape(1, cells_x, columns)
    pencil, pencil_weight = (
        lax.all_to_all(stacked, "gx", split_axis=2, concat_axis=1, tiled=True),
        lax.all_to_all(weight_flat, "gx", split_axis=2, concat_axis=1, tiled=True),
    )
    smooth = filter_lines(pencil, filter_matrices)
    returned = pencil + pencil_weight * (smooth - pencil)
    back_lines = lax.all_to_all(returned, "gx", split_axis=1, concat_axis=2, tiled=True)
    conserved_next = back_lines.reshape(5, cells_x, span, cells_y)
    partial_histogram = plane_histogram(shock_sensor, dilatation_bin, vorticity_bin)
    summed = lax.psum(partial_histogram, ("gx", "gy"))
    all_cells = cells_x * slab_count * span * total_y
    histogram = summed * (HISTOGRAM_BINS * HISTOGRAM_BINS / all_cells)
    return (conserved_next, histogram)


def solution(mesh):
    in_specs = (
        P("gx", None, "gy"),
        P(None, "gx", None, "gy"),
        P("gx", None, "gy"),
        P("gx"),
        P("gx"),
        P("gx", None),
        P("gx"),
        P(),
        P(None, "gy"),
        P("gx", None, "gy"),
        P("gx", None, "gy"),
    )
    out_specs = (P(None, "gx", None, "gy"), P())
    return jax.shard_map(shards, mesh=mesh, in_specs=in_specs, out_specs=out_specs, check_vma=False)
```

profile of v0, /device:TPU:0, one launch (start us, length us, event | category | flops | bytes accessed | tf_op | source)
XLA Modules:
  0.0 215.9 jit_solution(9551707045615207745)
XLA Ops:
  0.6 0.9 pad_maximum_fusion.4
  1.6 1.3 collective-permute-start.1
  2.9 5.5 %collective-permute-start = (f32[5,1,32,32]{3,2,0,1:T(8,128)S(1)}, f32[5,1,32,32]{3,2,0,1:T(8,128)S(1)}, u32[]{:S(2)}, u32[]{:S(2)}) collective-permute-start(f32[5,1,32,32]{3,2,0,1:T(8,128)S(1)} %get-tuple-element.222), channel_id=1, source_target_pairs={{0,2},{2,4},{4,6},{6,8},{8,10},{10,12},{12,14},{14,16},{16,18},{18... | collective-permute-start | bytes 61448 | tf_op jit(solution)/shard_map/ppermute | solution.py:23
  8.4 0.7 convert_element_type.33
  9.1 0.7 convert_element_type.31
  9.7 0.7 multiply_multiply_fusion
  10.8 75.6 %psum.14 = f32[3,32,32]{2,1,0:T(8,128)S(1)} all-reduce(f32[3,32,32]{2,1,0:T(8,128)S(1)} %fusion.50), channel_id=1, replica_groups=mesh['gx'=16,'gy'=2] {'gx'}, use_global_device_ids=true, to_apply=%region_1.2 | all-reduce | flops 3072 | bytes 24576 | tf_op jit(solution)/shard_map/psum | solution.py:153
  86.4 1.2 pad_maximum_fusion.2
  87.6 0.7 convert_bitcast_fusion
  88.4 0.6 slice.495
  88.9 1.2 pad_maximum_fusion
  91.2 1.3 collective-permute-start.3
  92.5 3.0 %collective-permute-start.2 = (f32[5,10,32,1]{2,3,1,0:T(1,128)S(1)}, f32[5,10,32,1]{2,3,1,0:T(1,128)S(1)}, u32[]{:S(2)}, u32[]{:S(2)}) collective-permute-start(f32[5,10,32,1]{2,3,1,0:T(1,128)S(1)} %copy.81), channel_id=1, source_target_pairs={{0,1},{2,3},{4,5},{6,7},{8,9},{10,11},{12,13},{14,15},{16,17},{18,... | collective-permute-start | bytes 19208 | tf_op jit(solution)/shard_map/ppermute | solution.py:23
  95.5 1.4 and_reduce_fusion
  96.9 0.4 copy.83
  97.3 1.3 copy.84
  98.6 1.6 pad_maximum_fusion.1
  100.2 1.4 fusion.48
  101.6 1.7 scatter.14
  103.4 1.0 scatter.15
  104.5 0.9 scatter.16
  105.4 0.4 slice_select_fusion
  105.9 3.7 %scatter.19 = f32[5,10,32,34]{3,2,0,1:T(8,128)S(1)} dynamic-update-slice(f32[5,10,32,34]{3,2,0,1:T(8,128)S(1)} %scatter.16, f32[5,8,32,1]{3,2,0,1:T(8,128)S(1)} %slice_select_fusion, s32[]{:T(128)} %constant.328.clone.1, s32[]{:T(128)} %constant.350.clone.1, s32[]{:T(128)} %constant.328.clone.1, s32[]{:T(128)} %constant.351.clone.1) | dynamic-update-slice | bytes 10244 | tf_op jit(solution)/shard_map/scatter | solution.py:165
  111.2 1.2 fusion.91
  112.4 0.4 broadcast_multiply_fusion.3
  112.8 1.0 copy.119
  113.9 0.5 broadcast.273
  114.4 3.7 %reduce.27 = f32[1024,8]{1,0:T(8,128)} reduce(f32[1024,1,8]{2,1,0:T(1,128)} %bitcast.128, f32[]{:T(128)} %broadcast.273), dimensions={1}, to_apply=%bitcast.110.reduce_sub_computation | reduce | bytes 65540
  118.1 1.9 reshape.467
  120.0 3.5 %all-to-all-start.1 = ((f32[16,1,512]{2,1,0:T(1,128)}), f32[16,1,512]{2,1,0:T(1,128)S(1)}, u32[]{:S(2)}, u32[]{:S(2)}) async-start(f32[16,1,512]{2,1,0:T(1,128)} %reshape.467), calls=%async_computation.1 | async-start | bytes 65536 | tf_op jit(solution)/shard_map/all_to_all | solution.py:180
  123.5 2.7 %fusion.14 = f32[5,8,32,32]{3,2,0,1:T(8,128)} fusion(f32[5,10,32,34]{3,2,0,1:T(8,128)S(1)} %get-tuple-element.221, f32[5,10,32,34]{3,2,0,1:T(8,128)S(1)} %scatter.19, f32[5,8,1,32]{3,2,0,1:T(1,128)S(1)} %get-tuple-element.213, f32[5,8,31,32]{3,2,0,1:T(8,128)} %get-tuple-element.215, f32[5,8,31,32]{3,2,0,1:T(8,128)S(1)} %get-tuple-element.214, ...), kind=kLoop, calls=%fused_computation.23 | loop fusion | flops 368640 | bytes 4295680 | tf_op jit(solution)/shard_map/sub | solution.py:75
  126.2 3.6 %copy.122 = f32[5,8,32,32]{1,0,3,2:T(8,128)} copy(f32[5,8,32,32]{3,2,0,1:T(8,128)} %fusion.14) | data formatting | bytes 327680 | tf_op jit(solution)/shard_map/reshape | solution.py:176
  129.8 3.4 %reshape.465 = f32[16,1,2560]{2,1,0:T(1,128)} reshape(f32[1024,5,8]{2,1,0:T(8,128)} %bitcast.117) | data formatting | bytes 327680
  133.1 6.9 %all-to-all-start = ((f32[16,1,2560]{2,1,0:T(1,128)}), f32[16,1,2560]{2,1,0:T(1,128)S(1)}, u32[]{:S(2)}, u32[]{:S(2)}) async-start(f32[16,1,2560]{2,1,0:T(1,128)} %reshape.465), calls=%async_computation | async-start | bytes 327680 | tf_op jit(solution)/shard_map/all_to_all | solution.py:179
  140.0 0.6 reduce.28
  140.7 0.9 reshape.468
  141.8 6.1 %all-to-all-done = f32[16,1,2560]{2,1,0:T(1,128)S(1)} async-done(((f32[16,1,2560]{2,1,0:T(1,128)}), f32[16,1,2560]{2,1,0:T(1,128)S(1)}, u32[]{:S(2)}, u32[]{:S(2)}) %all-to-all-start) | async-done | bytes 163872 | tf_op jit(solution)/shard_map/all_to_all | solution.py:179
  147.9 0.9 reduce.26
  148.9 2.6 %reshape.466 = f32[1024,5,8]{2,1,0:T(8,128)} reshape(f32[16,2560]{1,0:T(8,128)S(1)} %reduce.26) | data formatting | bytes 327680
  151.5 2.6 %copy.103 = f32[5,16,8,64]{3,2,1,0:T(8,128)S(1)} copy(f32[5,16,8,64]{2,0,3,1:T(8,128)} %bitcast.118) | data formatting | bytes 327680 | tf_op jit(solution)/shard_map/all_to_all | solution.py:179
  154.2 0.7 fusion.10
  155.2 0.9 reshape.469
  156.1 3.5 %all-to-all-start.2 = ((f32[16,1,2560]{2,1,0:T(1,128)}), f32[16,1,2560]{2,1,0:T(1,128)S(1)}, u32[]{:S(2)}, u32[]{:S(2)}) async-start(f32[16,1,2560]{2,1,0:T(1,128)} %reshape.469), calls=%async_computation.2 | async-start | bytes 327680 | tf_op jit(solution)/shard_map/all_to_all | solution.py:184
  159.6 12.6 %while.22 = (s32[]{:T(128)}, f32[64,64]{1,0:T(8,128)S(1)}, s32[8,32,32]{2,1,0:T(8,128)}, s32[8,32,32]{2,1,0:T(8,128)}, f32[8,32,32]{2,1,0:T(8,128)S(1)}, /*index=5*/s32[]{:T(128)}, s32[]{:T(128)}) while((s32[]{:T(128)}, f32[64,64]{1,0:T(8,128)S(1)}, s32[8,32,32]{2,1,0:T(8,128)}, s32[8,32,32]{2,1,0:T(8,128)}, ...), condition=%wide.region_4.5_spmd.clone.clone, body=%wide.region_3.4_spmd.clone.clone.sunk | while | flops 50536448 | bytes 94311 | solution.py:113
  159.7 0.7 constant_dynamic-slice_fusion.6
  160.6 0.6 convolution_add_fusion.2
  161.3 0.7 constant_dynamic-slice_fusion.6
  162.2 0.6 convolution_add_fusion.2
  162.8 0.7 constant_dynamic-slice_fusion.6
  163.7 0.6 convolution_add_fusion.2
  164.4 0.7 constant_dynamic-slice_fusion.6
  165.3 0.6 convolution_add_fusion.2
  166.0 0.7 constant_dynamic-slice_fusion.6
  166.9 0.6 convolution_add_fusion.2
  167.6 0.7 constant_dynamic-slice_fusion.6
  168.5 0.6 convolution_add_fusion.2
  169.1 0.7 constant_dynamic-slice_fusion.6
  170.0 0.6 convolution_add_fusion.2
  170.7 0.7 constant_dynamic-slice_fusion.6
  171.6 0.6 convolution_add_fusion.2
  172.2 40.8 %psum.15 = f32[64,64]{1,0:T(8,128)S(1)} all-reduce(f32[64,64]{1,0:T(8,128)S(1)} %get-tuple-element.157), channel_id=1, replica_groups=mesh['gx'=16,'gy'=2] {'gx','gy'}, use_global_device_ids=true, to_apply=%region_5.6 | all-reduce | flops 4096 | bytes 32768 | tf_op jit(solution)/shard_map/psum | solution.py:187
  213.0 0.6 broadcast_multiply_fusion.4
  213.6 0.9 reduce.29
  214.9 1.0 reshape.460
  (85 shorter events, 6.0 us)
Async XLA Ops:
  0.6 153.6 %copy-start = (f32[1,128,128]{2,1,0:T(8,128)S(1)}, f32[1,128,128]{2,1,0:T(8,128)}, u32[]{:S(2)}) copy-start(f32[1,128,128]{2,1,0:T(8,128)} %param.40) | copy-start | bytes 196612
  1.6 93.9 %copy-start.4 = (s32[4]{0:T(128)S(1)}, s32[4]{0:T(128)}, u32[]{:S(2)}) copy-start(s32[4]{0:T(128)} %constant.330.clone.1) | copy-start | bytes 52
  1.6 87.3 %collective-permute-start.1 = (f32[5,1,32,32]{3,2,0,1:T(8,128)S(1)}, f32[5,1,32,32]{3,2,0,1:T(8,128)S(1)}, u32[]{:S(2)}, u32[]{:S(2)}) collective-permute-start(f32[5,1,32,32]{3,2,0,1:T(8,128)S(1)} %get-tuple-element.223), channel_id=1, source_target_pairs={{2,0},{4,2},{6,4},{8,6},{10,8},{12,10},{14,12},{16,14},{18,16},{20... | collective-permute-start | bytes 61448 | tf_op jit(solution)/shard_map/ppermute | solution.py:24
  2.9 86.0 %collective-permute-start = (f32[5,1,32,32]{3,2,0,1:T(8,128)S(1)}, f32[5,1,32,32]{3,2,0,1:T(8,128)S(1)}, u32[]{:S(2)}, u32[]{:S(2)}) collective-permute-start(f32[5,1,32,32]{3,2,0,1:T(8,128)S(1)} %get-tuple-element.222), channel_id=1, source_target_pairs={{0,2},{2,4},{4,6},{6,8},{8,10},{10,12},{12,14},{14,16},{16,18},{18... | collective-permute-start | bytes 61448 | tf_op jit(solution)/shard_map/ppermute | solution.py:23
  87.6 11.0 %copy-start.1 = (f32[3,8,32,32]{3,2,1,0:T(8,128)S(1)}, f32[3,8,32,32]{3,2,1,0:T(8,128)}, u32[]{:S(2)}) copy-start(f32[3,8,32,32]{3,2,1,0:T(8,128)} %param.34) | copy-start | bytes 294916
  87.6 11.0 %copy-start.2 = (f32[8,32,32]{2,1,0:T(8,128)S(1)}, f32[8,32,32]{2,1,0:T(8,128)}, u32[]{:S(2)}) copy-start(f32[8,32,32]{2,1,0:T(8,128)} %param.35) | copy-start | bytes 98308
  87.6 11.0 %copy-start.3 = (f32[8,32,32]{2,1,0:T(8,128)S(1)}, f32[8,32,32]{2,1,0:T(8,128)}, u32[]{:S(2)}) copy-start(f32[8,32,32]{2,1,0:T(8,128)} %param.33) | copy-start | bytes 98308
  91.2 6.1 %collective-permute-start.3 = (f32[5,10,32,1]{2,3,1,0:T(1,128)S(1)}, f32[5,10,32,1]{2,3,1,0:T(1,128)S(1)}, u32[]{:S(2)}, u32[]{:S(2)}) collective-permute-start(f32[5,10,32,1]{2,3,1,0:T(1,128)S(1)} %copy.82), channel_id=1, source_target_pairs={{1,0},{3,2},{5,4},{7,6},{9,8},{11,10},{13,12},{15,14},{17,16},{19,... | collective-permute-start | bytes 19208 | tf_op jit(solution)/shard_map/ppermute | solution.py:24
  92.5 4.4 %collective-permute-start.2 = (f32[5,10,32,1]{2,3,1,0:T(1,128)S(1)}, f32[5,10,32,1]{2,3,1,0:T(1,128)S(1)}, u32[]{:S(2)}, u32[]{:S(2)}) collective-permute-start(f32[5,10,32,1]{2,3,1,0:T(1,128)S(1)} %copy.81), channel_id=1, source_target_pairs={{0,1},{2,3},{4,5},{6,7},{8,9},{10,11},{12,13},{14,15},{16,17},{18,... | collective-permute-start | bytes 19208 | tf_op jit(solution)/shard_map/ppermute | solution.py:23
  120.0 13.2 %all-to-all-start.1 = ((f32[16,1,512]{2,1,0:T(1,128)}), f32[16,1,512]{2,1,0:T(1,128)S(1)}, u32[]{:S(2)}, u32[]{:S(2)}) async-start(f32[16,1,512]{2,1,0:T(1,128)} %reshape.467), calls=%async_computation.1 | async-start | bytes 65536 | tf_op jit(solution)/shard_map/all_to_all | solution.py:180
  133.1 14.8 %all-to-all-start = ((f32[16,1,2560]{2,1,0:T(1,128)}), f32[16,1,2560]{2,1,0:T(1,128)S(1)}, u32[]{:S(2)}, u32[]{:S(2)}) async-start(f32[16,1,2560]{2,1,0:T(1,128)} %reshape.465), calls=%async_computation | async-start | bytes 327680 | tf_op jit(solution)/shard_map/all_to_all | solution.py:179
  156.1 57.5 %all-to-all-start.2 = ((f32[16,1,2560]{2,1,0:T(1,128)}), f32[16,1,2560]{2,1,0:T(1,128)S(1)}, u32[]{:S(2)}, u32[]{:S(2)}) async-start(f32[16,1,2560]{2,1,0:T(1,128)} %reshape.469), calls=%async_computation.2 | async-start | bytes 327680 | tf_op jit(solution)/shard_map/all_to_all | solution.py:184
where the time goes:
time: 218 us; the launch traced here: 216 us
  blocking collectives  116 us (53%)
  local copies, waits for them, and re-layouts  39.7 us (18%)
  starting transfers between devices  25 us (11%)
  other arithmetic  21.8 us (10%)
  waiting for transfers between devices  6.13 us (3%)
  matrix products  5.55 us (3%)
    psum x1, blocking collectives, shards(): inflow = lax.psum(partial_sum, 'gx')  75.6 us
    psum x1, blocking collectives, shards(): summed = lax.psum(partial_histogram, ('gx', 'gy'))  40.8 us
    unnamed x16, local copies, waits for them, and re-layouts  9.82 us
    ppermute x2, starting transfers between devices, extended(): before = lax.ppermute(last, axis, up)  8.5 us
    all_to_all x1, starting transfers between devices, shards(): lax.all_to_all(stacked, 'gx', split_axis=2, concat_axis=1, tiled=True)  6.88 us
    all_to_all x1, waiting for transfers between devices, shards(): lax.all_to_all(stacked, 'gx', split_axis=2, concat_axis=1, tiled=True)  6.11 us
    dynamic_slice x16, local copies, waits for them, and re-layouts, plane_histogram(): lax.scan(accumulate_plane, jnp.zeros((HISTOGRAM_BINS, HISTOGRAM_BINS), jn...  6 us
    dot_general x8, matrix products, accumulate_plane(): jnp.dot(dilatation_table, vorticity_table, precision=lax.Precision.HIGHEST)  4.61 us
  transfers between devices with their start and end apart: 7, of which 1 were waited for; matrix products, arithmetic and copies ran while one was open for 14% of the time, Pallas kernels for 0%

commit v1 on v0

--- a/solution.py
+++ b/solution.py
@@ -184,7 +184,7 @@
     back_lines = lax.all_to_all(returned, "gx", split_axis=1, concat_axis=2, tiled=True)
     conserved_next = back_lines.reshape(5, cells_x, span, cells_y)
     partial_histogram = plane_histogram(shock_sensor, dilatation_bin, vorticity_bin)
-    summed = lax.psum(partial_histogram, ("gx", "gy"))
+    summed = jnp.sum(lax.all_gather(partial_histogram, ("gx", "gy")), axis=0)
     all_cells = cells_x * slab_count * span * total_y
     histogram = summed * (HISTOGRAM_BINS * HISTOGRAM_BINS / all_cells)
     return (conserved_next, histogram)

time: 218 us -> 219 us (level)
  waiting for transfers between devices: 6.13 us -> 0.03 us
  blocking collectives: 116 us -> 120 us
  starting transfers between devices: 25 us -> 28.4 us
    all_gather x0 -> x1, blocking collectives: none -> 44.6 us  [shards(): summed = jnp.sum(lax.all_gather(partial_histogram, ('gx', 'gy')), axis=0)]
    psum x1 -> x0, blocking collectives: 40.8 us -> none  [shards(): summed = lax.psum(partial_histogram, ('gx', 'gy'))]
    all_to_all x1, waiting for transfers between devices: 6.11 us -> 0.01 us  [shards(): lax.all_to_all(stacked, 'gx', split_axis=2, concat_axis=1, tiled=True)]
    all_to_all x1, starting transfers between devices: 3.52 us -> 6.9 us  [shards(): lax.all_to_all(returned, 'gx', split_axis=1, concat_axis=2, tiled=True)]
  transfers between devices with their start and end apart: 7 -> 7, of which waited for: 1 -> 0; matrix products, arithmetic and copies ran while one was open for 14% -> 14% of each run, Pallas kernels for 0% -> 0%
where the time goes in v1:
time: 219 us; the launch traced here: 217 us
  blocking collectives  120 us (55%)
  local copies, waits for them, and re-layouts  39.7 us (18%)
  starting transfers between devices  28.4 us (13%)
  other arithmetic  21.9 us (10%)
  matrix products  5.55 us (3%)
    psum x1, blocking collectives, shards(): inflow = lax.psum(partial_sum, 'gx')  75.6 us
    all_gather x1, blocking collectives, shards(): summed = jnp.sum(lax.all_gather(partial_histogram, ('gx', 'gy')), axis=0)  44.6 us
    unnamed x16, local copies, waits for them, and re-layouts  9.82 us
    ppermute x2, starting transfers between devices, extended(): before = lax.ppermute(last, axis, up)  8.5 us
    all_to_all x1, starting transfers between devices, shards(): lax.all_to_all(returned, 'gx', split_axis=1, concat_axis=2, tiled=True)  6.9 us
    all_to_all x1, starting transfers between devices, shards(): lax.all_to_all(stacked, 'gx', split_axis=2, concat_axis=1, tiled=True)  6.88 us
    dynamic_slice x16, local copies, waits for them, and re-layouts, plane_histogram(): lax.scan(accumulate_plane, jnp.zeros((HISTOGRAM_BINS, HISTOGRAM_BINS), jn...  5.97 us
    dot_general x8, matrix products, accumulate_plane(): jnp.dot(dilatation_table, vorticity_table, precision=lax.Precision.HIGHEST)  4.61 us
  transfers between devices with their start and end apart: 7, of which 0 were waited for; matrix products, arithmetic and copies ran while one was open for 14% of the time, Pallas kernels for 0%

profile of v1, /device:TPU:0, one launch (start us, length us, event | category | flops | bytes accessed | tf_op | source)
XLA Modules:
  0.0 217.1 jit_solution(7486132180842037127)
XLA Ops:
  0.6 0.9 pad_maximum_fusion.4
  1.6 1.3 collective-permute-start.1
  2.9 5.5 %collective-permute-start = (f32[5,1,32,32]{3,2,0,1:T(8,128)S(1)}, f32[5,1,32,32]{3,2,0,1:T(8,128)S(1)}, u32[]{:S(2)}, u32[]{:S(2)}) collective-permute-start(f32[5,1,32,32]{3,2,0,1:T(8,128)S(1)} %get-tuple-element.222), channel_id=1, source_target_pairs={{0,2},{2,4},{4,6},{6,8},{8,10},{10,12},{12,14},{14,16},{16,18},{18... | collective-permute-start | bytes 61448 | tf_op jit(solution)/shard_map/ppermute | solution.py:23
  8.4 0.7 convert_element_type.33
  9.1 0.7 convert_element_type.31
  9.7 0.7 multiply_multiply_fusion
  10.8 75.6 %psum.7 = f32[3,32,32]{2,1,0:T(8,128)S(1)} all-reduce(f32[3,32,32]{2,1,0:T(8,128)S(1)} %fusion.50), channel_id=1, replica_groups=mesh['gx'=16,'gy'=2] {'gx'}, use_global_device_ids=true, to_apply=%region_1.2 | all-reduce | flops 3072 | bytes 24576 | tf_op jit(solution)/shard_map/psum | solution.py:153
  86.4 1.2 pad_maximum_fusion.2
  87.6 0.7 convert_bitcast_fusion
  88.4 0.6 slice.495
  88.9 1.2 pad_maximum_fusion
  90.8 0.4 copy.82
  91.2 1.3 collective-permute-start.3
  92.5 3.0 %collective-permute-start.2 = (f32[5,10,32,1]{2,3,1,0:T(1,128)S(1)}, f32[5,10,32,1]{2,3,1,0:T(1,128)S(1)}, u32[]{:S(2)}, u32[]{:S(2)}) collective-permute-start(f32[5,10,32,1]{2,3,1,0:T(1,128)S(1)} %copy.81), channel_id=1, source_target_pairs={{0,1},{2,3},{4,5},{6,7},{8,9},{10,11},{12,13},{14,15},{16,17},{18,... | collective-permute-start | bytes 19208 | tf_op jit(solution)/shard_map/ppermute | solution.py:23
  95.5 1.4 and_reduce_fusion
  96.9 0.4 copy.83
  97.3 1.3 copy.84
  98.6 1.6 pad_maximum_fusion.1
  100.2 1.4 fusion.48
  101.6 1.7 scatter.14
  103.4 1.0 scatter.15
  104.5 0.9 scatter.16
  105.4 0.4 slice_select_fusion
  105.9 3.7 %scatter.19 = f32[5,10,32,34]{3,2,0,1:T(8,128)S(1)} dynamic-update-slice(f32[5,10,32,34]{3,2,0,1:T(8,128)S(1)} %scatter.16, f32[5,8,32,1]{3,2,0,1:T(8,128)S(1)} %slice_select_fusion, s32[]{:T(128)} %constant.328.clone.1, s32[]{:T(128)} %constant.350.clone.1, s32[]{:T(128)} %constant.328.clone.1, s32[]{:T(128)} %constant.351.clone.1) | dynamic-update-slice | bytes 10244 | tf_op jit(solution)/shard_map/scatter | solution.py:165
  111.2 1.2 fusion.91
  112.4 0.4 broadcast_multiply_fusion.3
  112.8 1.0 copy.119
  113.9 0.5 broadcast.273
  114.4 3.7 %reduce.27 = f32[1024,8]{1,0:T(8,128)} reduce(f32[1024,1,8]{2,1,0:T(1,128)} %bitcast.130, f32[]{:T(128)} %broadcast.273), dimensions={1}, to_apply=%bitcast.111.reduce_sub_computation | reduce | bytes 65540
  118.1 1.9 reshape.468
  120.0 3.5 %all-to-all-start.1 = ((f32[16,1,512]{2,1,0:T(1,128)}), f32[16,1,512]{2,1,0:T(1,128)S(1)}, u32[]{:S(2)}, u32[]{:S(2)}) async-start(f32[16,1,512]{2,1,0:T(1,128)} %reshape.468), calls=%async_computation.1 | async-start | bytes 65536 | tf_op jit(solution)/shard_map/all_to_all | solution.py:180
  123.5 2.7 %fusion.14 = f32[5,8,32,32]{3,2,0,1:T(8,128)} fusion(f32[5,10,32,34]{3,2,0,1:T(8,128)S(1)} %get-tuple-element.221, f32[5,10,32,34]{3,2,0,1:T(8,128)S(1)} %scatter.19, f32[5,8,1,32]{3,2,0,1:T(1,128)S(1)} %get-tuple-element.213, f32[5,8,31,32]{3,2,0,1:T(8,128)} %get-tuple-element.215, f32[5,8,31,32]{3,2,0,1:T(8,128)S(1)} %get-tuple-element.214, ...), kind=kLoop, calls=%fused_computation.23 | loop fusion | flops 368640 | bytes 4295680 | tf_op jit(solution)/shard_map/sub | solution.py:75
  126.2 3.6 %copy.122 = f32[5,8,32,32]{1,0,3,2:T(8,128)} copy(f32[5,8,32,32]{3,2,0,1:T(8,128)} %fusion.14) | data formatting | bytes 327680 | tf_op jit(solution)/shard_map/reshape | solution.py:176
  129.8 3.4 %reshape.466 = f32[16,1,2560]{2,1,0:T(1,128)} reshape(f32[1024,5,8]{2,1,0:T(8,128)} %bitcast.118) | data formatting | bytes 327680
  133.1 6.9 %all-to-all-start = ((f32[16,1,2560]{2,1,0:T(1,128)}), f32[16,1,2560]{2,1,0:T(1,128)S(1)}, u32[]{:S(2)}, u32[]{:S(2)}) async-start(f32[16,1,2560]{2,1,0:T(1,128)} %reshape.466), calls=%async_computation | async-start | bytes 327680 | tf_op jit(solution)/shard_map/all_to_all | solution.py:179
  140.0 12.6 %while.22 = (s32[]{:T(128)}, f32[64,64]{1,0:T(8,128)S(1)}, s32[8,32,32]{2,1,0:T(8,128)}, s32[8,32,32]{2,1,0:T(8,128)}, f32[8,32,32]{2,1,0:T(8,128)S(1)}, /*index=5*/s32[]{:T(128)}, s32[]{:T(128)}) while((s32[]{:T(128)}, f32[64,64]{1,0:T(8,128)S(1)}, s32[8,32,32]{2,1,0:T(8,128)}, s32[8,32,32]{2,1,0:T(8,128)}, ...), condition=%wide.region_4.5_spmd.clone.clone, body=%wide.region_3.4_spmd.clone.clone.sunk | while | flops 50536448 | bytes 94311 | solution.py:113
  140.1 0.7 constant_dynamic-slice_fusion.6
  141.0 0.6 convolution_add_fusion.2
  141.7 0.7 constant_dynamic-slice_fusion.6
  142.6 0.6 convolution_add_fusion.2
  143.3 0.7 constant_dynamic-slice_fusion.6
  144.2 0.6 convolution_add_fusion.2
  144.8 0.7 constant_dynamic-slice_fusion.6
  145.7 0.6 convolution_add_fusion.2
  146.4 0.7 constant_dynamic-slice_fusion.6
  147.3 0.6 convolution_add_fusion.2
  148.0 0.7 constant_dynamic-slice_fusion.6
  148.9 0.6 convolution_add_fusion.2
  149.6 0.7 constant_dynamic-slice_fusion.6
  150.4 0.6 convolution_add_fusion.2
  151.1 0.7 constant_dynamic-slice_fusion.6
  152.0 0.6 convolution_add_fusion.2
  152.6 0.6 reduce.28
  153.3 0.9 reshape.469
  154.4 0.9 reduce.26
  155.4 2.6 %reshape.467 = f32[1024,5,8]{2,1,0:T(8,128)} reshape(f32[16,2560]{1,0:T(8,128)S(1)} %reduce.26) | data formatting | bytes 327680
  158.0 2.6 %copy.103 = f32[5,16,8,64]{3,2,1,0:T(8,128)S(1)} copy(f32[5,16,8,64]{2,0,3,1:T(8,128)} %bitcast.119) | data formatting | bytes 327680 | tf_op jit(solution)/shard_map/all_to_all | solution.py:179
  160.7 0.7 fusion.10
  161.7 0.9 reshape.470
  162.6 6.9 %all-to-all-start.2 = ((f32[16,1,2560]{2,1,0:T(1,128)}), f32[16,1,2560]{2,1,0:T(1,128)S(1)}, u32[]{:S(2)}, u32[]{:S(2)}) async-start(f32[16,1,2560]{2,1,0:T(1,128)} %reshape.470), calls=%async_computation.2 | async-start | bytes 327680 | tf_op jit(solution)/shard_map/all_to_all | solution.py:184
  169.5 44.6 %all-gather = f32[2048,64]{1,0:T(8,128)S(1)} all-gather(f32[64,64]{1,0:T(8,128)S(1)} %get-tuple-element.157), channel_id=2, replica_groups=mesh['gx'=16,'gy'=2] {'gx','gy'}, dimensions={0}, use_global_device_ids=true | all-gather | bytes 540672 | tf_op jit(solution)/shard_map/all_gather | solution.py:187
  214.2 0.6 broadcast_multiply_fusion.4
  214.8 0.9 reduce.29
  216.1 1.0 reshape.460
  (86 shorter events, 5.7 us)
Async XLA Ops:
  0.6 160.1 %copy-start = (f32[1,128,128]{2,1,0:T(8,128)S(1)}, f32[1,128,128]{2,1,0:T(8,128)}, u32[]{:S(2)}) copy-start(f32[1,128,128]{2,1,0:T(8,128)} %param.40) | copy-start | bytes 196612
  1.6 93.9 %copy-start.4 = (s32[4]{0:T(128)S(1)}, s32[4]{0:T(128)}, u32[]{:S(2)}) copy-start(s32[4]{0:T(128)} %constant.330.clone.1) | copy-start | bytes 52
  1.6 87.3 %collective-permute-start.1 = (f32[5,1,32,32]{3,2,0,1:T(8,128)S(1)}, f32[5,1,32,32]{3,2,0,1:T(8,128)S(1)}, u32[]{:S(2)}, u32[]{:S(2)}) collective-permute-start(f32[5,1,32,32]{3,2,0,1:T(8,128)S(1)} %get-tuple-element.223), channel_id=1, source_target_pairs={{2,0},{4,2},{6,4},{8,6},{10,8},{12,10},{14,12},{16,14},{18,16},{20... | collective-permute-start | bytes 61448 | tf_op jit(solution)/shard_map/ppermute | solution.py:24
  2.9 86.0 %collective-permute-start = (f32[5,1,32,32]{3,2,0,1:T(8,128)S(1)}, f32[5,1,32,32]{3,2,0,1:T(8,128)S(1)}, u32[]{:S(2)}, u32[]{:S(2)}) collective-permute-start(f32[5,1,32,32]{3,2,0,1:T(8,128)S(1)} %get-tuple-element.222), channel_id=1, source_target_pairs={{0,2},{2,4},{4,6},{6,8},{8,10},{10,12},{12,14},{14,16},{16,18},{18... | collective-permute-start | bytes 61448 | tf_op jit(solution)/shard_map/ppermute | solution.py:23
  87.6 11.0 %copy-start.1 = (f32[3,8,32,32]{3,2,1,0:T(8,128)S(1)}, f32[3,8,32,32]{3,2,1,0:T(8,128)}, u32[]{:S(2)}) copy-start(f32[3,8,32,32]{3,2,1,0:T(8,128)} %param.34) | copy-start | bytes 294916
  87.6 11.0 %copy-start.2 = (f32[8,32,32]{2,1,0:T(8,128)S(1)}, f32[8,32,32]{2,1,0:T(8,128)}, u32[]{:S(2)}) copy-start(f32[8,32,32]{2,1,0:T(8,128)} %param.35) | copy-start | bytes 98308
  87.6 11.0 %copy-start.3 = (f32[8,32,32]{2,1,0:T(8,128)S(1)}, f32[8,32,32]{2,1,0:T(8,128)}, u32[]{:S(2)}) copy-start(f32[8,32,32]{2,1,0:T(8,128)} %param.33) | copy-start | bytes 98308
  91.2 6.1 %collective-permute-start.3 = (f32[5,10,32,1]{2,3,1,0:T(1,128)S(1)}, f32[5,10,32,1]{2,3,1,0:T(1,128)S(1)}, u32[]{:S(2)}, u32[]{:S(2)}) collective-permute-start(f32[5,10,32,1]{2,3,1,0:T(1,128)S(1)} %copy.82), channel_id=1, source_target_pairs={{1,0},{3,2},{5,4},{7,6},{9,8},{11,10},{13,12},{15,14},{17,16},{19,... | collective-permute-start | bytes 19208 | tf_op jit(solution)/shard_map/ppermute | solution.py:24
  92.5 4.4 %collective-permute-start.2 = (f32[5,10,32,1]{2,3,1,0:T(1,128)S(1)}, f32[5,10,32,1]{2,3,1,0:T(1,128)S(1)}, u32[]{:S(2)}, u32[]{:S(2)}) collective-permute-start(f32[5,10,32,1]{2,3,1,0:T(1,128)S(1)} %copy.81), channel_id=1, source_target_pairs={{0,1},{2,3},{4,5},{6,7},{8,9},{10,11},{12,13},{14,15},{16,17},{18,... | collective-permute-start | bytes 19208 | tf_op jit(solution)/shard_map/ppermute | solution.py:23
  120.0 13.2 %all-to-all-start.1 = ((f32[16,1,512]{2,1,0:T(1,128)}), f32[16,1,512]{2,1,0:T(1,128)S(1)}, u32[]{:S(2)}, u32[]{:S(2)}) async-start(f32[16,1,512]{2,1,0:T(1,128)} %reshape.468), calls=%async_computation.1 | async-start | bytes 65536 | tf_op jit(solution)/shard_map/all_to_all | solution.py:180
  133.1 21.3 %all-to-all-start = ((f32[16,1,2560]{2,1,0:T(1,128)}), f32[16,1,2560]{2,1,0:T(1,128)S(1)}, u32[]{:S(2)}, u32[]{:S(2)}) async-start(f32[16,1,2560]{2,1,0:T(1,128)} %reshape.466), calls=%async_computation | async-start | bytes 327680 | tf_op jit(solution)/shard_map/all_to_all | solution.py:179
  162.6 52.3 %all-to-all-start.2 = ((f32[16,1,2560]{2,1,0:T(1,128)}), f32[16,1,2560]{2,1,0:T(1,128)S(1)}, u32[]{:S(2)}, u32[]{:S(2)}) async-start(f32[16,1,2560]{2,1,0:T(1,128)} %reshape.470), calls=%async_computation.2 | async-start | bytes 327680 | tf_op jit(solution)/shard_map/all_to_all | solution.py:184
